TPU v7x, 32 devices: a whole 2x2x4 slice. The times are simulated.
32 devices in a mesh: shard: 8 (over z, y), tensor: 4 (over x, core).
Axes of the slice: x: 2, y: 2, z: 4, core: 2. Of those that a mesh axis runs over, the one named last changes fastest.
Arguments:
- tokens: bfloat16 [12608, 1024], P('shard'), may hold values from -6 to 6
- cotangent: bfloat16 [12608, 1024], P('shard'), may hold values from -6 to 6
- input_weight: float32 [3, 1024, 1024], P(None, 'shard', 'tensor'), may hold values from -2 to 2
- input_moments: float32 [2, 3, 1024, 1024], P(None, None, 'shard', 'tensor'), may hold values from -1 to 1, as said below
- input_bias: float32 [2, 1024], P(None, ('tensor', 'shard')), may hold values from -3 to 3
- input_bias_moments: float32 [2, 2, 1024], P(None, None, ('tensor', 'shard')), may hold values from -1 to 1, as said below
- output_weight: float32 [1024, 1024], P('tensor', 'shard'), may hold values from -0.75 to 0.75
- output_moments: float32 [2, 1024, 1024], P(None, 'tensor', 'shard'), may hold values from -1 to 1, as said below
- expand_weight: float32 [1024, 4096], P('shard', 'tensor'), may hold values from -0.1875 to 0.1875
- expand_moments: float32 [2, 1024, 4096], P(None, 'shard', 'tensor'), may hold values from -1 to 1, as said below
- expand_bias: float32 [4096], P(('tensor', 'shard')), may hold values from -3 to 3
- expand_bias_moments: float32 [2, 4096], P(None, ('tensor', 'shard')), may hold values from -1 to 1, as said below
- shrink_weight: float32 [4096, 1024], P('tensor', 'shard'), may hold values from -0.09375 to 0.09375
- shrink_moments: float32 [2, 4096, 1024], P(None, 'tensor', 'shard'), may hold values from -1 to 1, as said below
- vectors: float32 [6, 1024], P(None, 'shard'), may hold values from -1.2 to 1.4
- vector_moments: float32 [2, 6, 1024], P(None, None, 'shard'), may hold values from -1 to 1, as said below
Outputs:
- block_output: bfloat16 [12608, 1024], P('shard')
- token_gradient: float32 [12608, 1024], P('shard')
- input_weight_gradient: float32 [3, 1024, 1024], P(None, 'shard', 'tensor')
- input_bias_gradient: float32 [2, 1024], P(None, ('tensor', 'shard'))
- output_weight_gradient: float32 [1024, 1024], P('tensor', 'shard')
- expand_weight_gradient: float32 [1024, 4096], P('shard', 'tensor')
- expand_bias_gradient: float32 [4096], P(('tensor', 'shard'))
- shrink_weight_gradient: float32 [4096, 1024], P('tensor', 'shard')
- vectors_gradient: float32 [6, 1024], P(None, 'shard')
- new_input_weight: float32 [3, 1024, 1024], P(None, 'shard', 'tensor')
- new_input_bias: float32 [2, 1024], P(None, ('tensor', 'shard'))
- new_output_weight: float32 [1024, 1024], P('tensor', 'shard')
- new_expand_weight: float32 [1024, 4096], P('shard', 'tensor')
- new_expand_bias: float32 [4096], P(('tensor', 'shard'))
- new_shrink_weight: float32 [4096, 1024], P('tensor', 'shard')
- new_vectors: float32 [6, 1024], P(None, 'shard')
- new_input_moments: float32 [2, 3, 1024, 1024], P(None, None, 'shard', 'tensor')
- new_input_bias_moments: float32 [2, 2, 1024], P(None, None, ('tensor', 'shard'))
- new_output_moments: float32 [2, 1024, 1024], P(None, 'tensor', 'shard')
- new_expand_moments: float32 [2, 1024, 4096], P(None, 'shard', 'tensor')
- new_expand_bias_moments: float32 [2, 4096], P(None, ('tensor', 'shard'))
- new_shrink_moments: float32 [2, 4096, 1024], P(None, 'tensor', 'shard')
- new_vector_moments: float32 [2, 6, 1024], P(None, None, 'shard')
Inputs may be any that keep to these rules, and one draw needn't show every extreme that they name: `input_moments`: second moments positive. `input_bias_moments`: second moments positive. `output_moments`: second moments positive. `expand_moments`: second moments positive. `expand_bias_moments`: second moments positive. `shrink_moments`: second moments positive. `vector_moments`: second moments positive.
All inputs are finite; a program needn't handle non-finite values.
Results may differ from a plain program's by a relative error of at most 0.015.
Values may be sent and summed in bfloat16 or wider, within the bound.
No kernel may reach another device: no remote copies, remote signals or barrier semaphores. Data moves between devices by JAX's collectives and lax.ppermute only.
A program may use at most 192 MiB of HBM per device.

v0:
```python
import jax
import jax.numpy as jnp
from jax import lax
from jax.sharding import PartitionSpec as P

HEAD = 64
SEQ = 197
norm_eps = 1e-06
rate = 0.003
first_decay = 0.9
second_decay = 0.95
weight_decay = 0.05
step_count = 2.0
adam_eps = 1e-08
loss_scale = 128.0


def layer_norm(values, gain, shift):
    row_mean = jnp.mean(values, axis=-1, keepdims=True)
    centred = values - row_mean
    spread = jnp.mean(centred * centred, axis=-1, keepdims=True)
    return centred * lax.rsqrt(spread + norm_eps) * gain + shift


def gelu_exact(values):
    return jax.nn.gelu(values, approximate=False)


def split_heads(values, images):
    return values.reshape(images, SEQ, values.shape[-1] // HEAD, HEAD)


def head_scores(query_heads, key_heads, scale):
    return (
        jnp.einsum("gqhe,gkhe->ghqk", query_heads, key_heads, preferred_element_type=jnp.float32)
        * scale
    )


def adamw(param, moments, grad, decay):
    scaled = grad / loss_scale
    first = first_decay * moments[0] + (1.0 - first_decay) * scaled
    second = second_decay * moments[1] + (1.0 - second_decay) * scaled * scaled
    corrected = (
        first
        / (1.0 - first_decay**step_count)
        / (jnp.sqrt(second / (1.0 - second_decay**step_count)) + adam_eps)
    )
    return (param - rate * (corrected + decay * param), jnp.stack([first, second]))


def on_device(
    tokens,
    cotangent,
    input_weight,
    input_moments,
    input_bias,
    input_bias_moments,
    output_weight,
    output_moments,
    expand_weight,
    expand_moments,
    expand_bias,
    expand_bias_moments,
    shrink_weight,
    shrink_moments,
    vectors,
    vector_moments,
):
    full_input, full_bias, full_output, full_expand, full_expand_bias, full_shrink, full_vectors = (
        lax.all_gather(input_weight.astype(jnp.bfloat16), "shard", axis=1, tiled=True),
        lax.all_gather(input_bias.astype(jnp.bfloat16), "shard", axis=1, tiled=True),
        lax.all_gather(output_weight.astype(jnp.bfloat16), "shard", axis=1, tiled=True),
        lax.all_gather(expand_weight.astype(jnp.bfloat16), "shard", axis=0, tiled=True),
        lax.all_gather(expand_bias.astype(jnp.bfloat16), "shard", axis=0, tiled=True),
        lax.all_gather(shrink_weight.astype(jnp.bfloat16), "shard", axis=1, tiled=True),
        lax.all_gather(vectors.astype(jnp.bfloat16), "shard", axis=1, tiled=True),
    )
    norm_vectors = full_vectors.astype(jnp.float32)
    bias_values = full_bias.astype(jnp.float32)
    rows = tokens.shape[0]
    images = rows // SEQ
    scale = HEAD ** (-0.5)
    start_tokens = tokens.astype(jnp.float32)
    normed, first_back = jax.vjp(layer_norm, start_tokens, norm_vectors[0], norm_vectors[1])
    inputs = normed.astype(jnp.bfloat16)
    project = jnp.einsum("rd,cde->cre", inputs, full_input, preferred_element_type=jnp.float32)
    query = (project[0] + bias_values[0]).astype(jnp.bfloat16)
    keys = project[1].astype(jnp.bfloat16)
    values = (project[2] + bias_values[1]).astype(jnp.bfloat16)
    query_heads = split_heads(query, images)
    key_heads = split_heads(keys, images)
    value_heads = split_heads(values, images)
    scores = head_scores(query_heads, key_heads, scale)
    top = jnp.max(scores, axis=-1, keepdims=True)
    raised = jnp.exp(scores - top)
    total = jnp.sum(raised, axis=-1, keepdims=True)
    attention = (raised / total).astype(jnp.bfloat16)
    log_total = top + jnp.log(total)
    context = jnp.einsum(
        "ghqk,gkhe->gqhe", attention, value_heads, preferred_element_type=jnp.float32
    )
    context = context.reshape(rows, -1).astype(jnp.bfloat16)
    mixed = lax.psum(jnp.dot(context, full_output, preferred_element_type=jnp.float32), "tensor")
    attended = start_tokens + mixed + norm_vectors[2]
    normed_mid, second_back = jax.vjp(layer_norm, attended, norm_vectors[3], norm_vectors[4])
    inputs_mid = normed_mid.astype(jnp.bfloat16)
    pre_act = jnp.dot(
        inputs_mid, full_expand, preferred_element_type=jnp.float32
    ) + full_expand_bias.astype(jnp.float32)
    activated, gelu_back = jax.vjp(gelu_exact, pre_act)
    hidden = activated.astype(jnp.bfloat16)
    shrink_term = jnp.dot(hidden, full_shrink, preferred_element_type=jnp.float32)
    shrunk = lax.psum(shrink_term.astype(jnp.bfloat16), "tensor").astype(jnp.float32)
    block_output = (attended + shrunk + norm_vectors[5]).astype(jnp.bfloat16)
    back_values = cotangent.astype(jnp.float32)
    grad_shrink = jnp.einsum("rf,rd->fd", hidden, cotangent, preferred_element_type=jnp.float32)
    hidden_grad = jnp.einsum(
        "rd,fd->rf", cotangent, full_shrink, preferred_element_type=jnp.float32
    )
    pre_grad = gelu_back(hidden_grad)[0].astype(jnp.bfloat16)
    grad_expand = jnp.einsum("rd,rf->df", inputs_mid, pre_grad, preferred_element_type=jnp.float32)
    grad_expand_bias = jnp.sum(pre_grad.astype(jnp.float32), axis=0)
    mid_part = jnp.einsum("rf,df->rd", pre_grad, full_expand, preferred_element_type=jnp.float32)
    mid_normed_grad = lax.psum(mid_part, "tensor")
    mid_from_norm, gain_two, shift_two = second_back(mid_normed_grad)
    mid_grad = back_values + mid_from_norm
    mid_low = mid_grad.astype(jnp.bfloat16)
    grad_output = jnp.einsum("rk,rd->kd", context, mid_low, preferred_element_type=jnp.float32)
    context_grad = jnp.einsum(
        "rd,kd->rk", mid_low, full_output, preferred_element_type=jnp.float32
    ).astype(jnp.bfloat16)
    context_heads = split_heads(context_grad, images)
    scores = head_scores(query_heads, key_heads, scale)
    probability = jnp.exp(scores - log_total)
    prob_low = probability.astype(jnp.bfloat16)
    prob_grad = jnp.einsum(
        "gqhe,gkhe->ghqk", context_heads, value_heads, preferred_element_type=jnp.float32
    )
    values_grad = jnp.einsum(
        "ghqk,gqhe->gkhe", prob_low, context_heads, preferred_element_type=jnp.float32
    )
    row_dot = jnp.sum(prob_grad * probability, axis=-1, keepdims=True)
    score_grad = (probability * (prob_grad - row_dot)).astype(jnp.bfloat16)
    query_grad = (
        jnp.einsum("ghqk,gkhe->gqhe", score_grad, key_heads, preferred_element_type=jnp.float32)
        * scale
    )
    keys_grad = (
        jnp.einsum("ghqk,gqhe->gkhe", score_grad, query_heads, preferred_element_type=jnp.float32)
        * scale
    )
    project_grad = jnp.stack(
        [query_grad.reshape(rows, -1), keys_grad.reshape(rows, -1), values_grad.reshape(rows, -1)]
    ).astype(jnp.bfloat16)
    grad_bias = jnp.stack(
        [
            jnp.sum(project_grad[0].astype(jnp.float32), axis=0),
            jnp.sum(project_grad[2].astype(jnp.float32), axis=0),
        ]
    )
    grad_input = jnp.einsum("rd,cre->cde", inputs, project_grad, preferred_element_type=jnp.float32)
    input_part = jnp.einsum(
        "cre,cde->rd", project_grad, full_input, preferred_element_type=jnp.float32
    )
    normed_grad = lax.psum(input_part.astype(jnp.bfloat16), "tensor").astype(jnp.float32)
    token_from_norm, gain_one, shift_one = first_back(normed_grad)
    token_gradient = mid_grad + token_from_norm
    grad_vectors = jnp.stack(
        [
            gain_one,
            shift_one,
            jnp.sum(mid_grad, axis=0),
            gain_two,
            shift_two,
            jnp.sum(back_values, axis=0),
        ]
    )
    (
        share_input,
        share_bias,
        share_output,
        share_expand,
        share_expand_bias,
        share_shrink,
        share_vectors,
    ) = (
        lax.psum_scatter(
            grad_input.astype(jnp.bfloat16), "shard", scatter_dimension=1, tiled=True
        ).astype(jnp.float32),
        lax.psum_scatter(
            grad_bias.astype(jnp.bfloat16), "shard", scatter_dimension=1, tiled=True
        ).astype(jnp.float32),
        lax.psum_scatter(
            grad_output.astype(jnp.bfloat16), "shard", scatter_dimension=1, tiled=True
        ).astype(jnp.float32),
        lax.psum_scatter(
            grad_expand.astype(jnp.bfloat16), "shard", scatter_dimension=0, tiled=True
        ).astype(jnp.float32),
        lax.psum_scatter(
            grad_expand_bias.astype(jnp.bfloat16), "shard", scatter_dimension=0, tiled=True
        ).astype(jnp.float32),
        lax.psum_scatter(
            grad_shrink.astype(jnp.bfloat16), "shard", scatter_dimension=1, tiled=True
        ).astype(jnp.float32),
        lax.psum_scatter(
            grad_vectors.astype(jnp.bfloat16), "shard", scatter_dimension=1, tiled=True
        ).astype(jnp.float32),
    )
    new_input, mom_input = adamw(input_weight, input_moments, share_input, weight_decay)
    new_bias, mom_bias = adamw(input_bias, input_bias_moments, share_bias, 0.0)
    new_output, mom_output = adamw(output_weight, output_moments, share_output, weight_decay)
    new_expand, mom_expand = adamw(expand_weight, expand_moments, share_expand, weight_decay)
    new_expand_bias, mom_expand_bias = adamw(
        expand_bias, expand_bias_moments, share_expand_bias, 0.0
    )
    new_shrink, mom_shrink = adamw(shrink_weight, shrink_moments, share_shrink, weight_decay)
    new_vectors, mom_vectors = adamw(vectors, vector_moments, share_vectors, 0.0)
    return (
        block_output,
        token_gradient,
        share_input,
        share_bias,
        share_output,
        share_expand,
        share_expand_bias,
        share_shrink,
        share_vectors,
        new_input,
        new_bias,
        new_output,
        new_expand,
        new_expand_bias,
        new_shrink,
        new_vectors,
        mom_input,
        mom_bias,
        mom_output,
        mom_expand,
        mom_expand_bias,
        mom_shrink,
        mom_vectors,
    )


def solution(mesh):
    return jax.shard_map(
        on_device,
        mesh=mesh,
        in_specs=(
            P("shard", None),
            P("shard", None),
            P(None, "shard", "tensor"),
            P(None, None, "shard", "tensor"),
            P(None, ("tensor", "shard")),
            P(None, None, ("tensor", "shard")),
            P("tensor", "shard"),
            P(None, "tensor", "shard"),
            P("shard", "tensor"),
            P(None, "shard", "tensor"),
            P(("tensor", "shard")),
            P(None, ("tensor", "shard")),
            P("tensor", "shard"),
            P(None, "tensor", "shard"),
            P(None, "shard"),
            P(None, None, "shard"),
        ),
        out_specs=(
            P("shard", None),
            P("shard", None),
            P(None, "shard", "tensor"),
            P(None, ("tensor", "shard")),
            P("tensor", "shard"),
            P("shard", "tensor"),
            P(("tensor", "shard")),
            P("tensor", "shard"),
            P(None, "shard"),
            P(None, "shard", "tensor"),
            P(None, ("tensor", "shard")),
            P("tensor", "shard"),
            P("shard", "tensor"),
            P(("tensor", "shard")),
            P("tensor", "shard"),
            P(None, "shard"),
            P(None, None, "shard", "tensor"),
            P(None, None, ("tensor", "shard")),
            P(None, "tensor", "shard"),
            P(None, "shard", "tensor"),
            P(None, ("tensor", "shard")),
            P(None, "tensor", "shard"),
            P(None, None, "shard"),
        ),
        check_vma=False,
    )
```

profile of v0, /device:TPU:0, one launch (start us, length us, event | category | flops | bytes accessed | tf_op | source)
XLA Modules:
  0.0 1107.1 jit_solution(8191705866244736395)
XLA Ops:
  10.5 22.3 %all-gather = bf16[8,32,2]{1,2,0:T(2,128)(2,1)S(1)} all-gather(bf16[1,32,2]{1,2,0:T(2,128)(2,1)S(1)} %convert_bitcast_fusion.1), channel_id=1, replica_groups=mesh['shard'=8,'tensor'=4] {'shard'}, dimensions={0}, use_global_device_ids=true | all-gather | bytes 1152 | tf_op jit(solution)/shard_map/all_gather | solution.py:72
  34.0 26.5 %all_gather.21 = bf16[6,1024]{1,0:T(8,128)(2,1)S(1)} all-gather(bf16[6,128]{1,0:T(8,128)(2,1)S(1)} %convert_element_type.150), channel_id=1, replica_groups=mesh['shard'=8,'tensor'=4] {'shard'}, dimensions={1}, use_global_device_ids=true | all-gather | bytes 13824 | tf_op jit(solution)/shard_map/all_gather | solution.py:77
  64.6 28.1 %all_gather.24 = bf16[256,1024]{1,0:T(8,128)(2,1)} all-gather(bf16[256,128]{1,0:T(8,128)(2,1)S(1)} %convert_element_type.163), channel_id=1, replica_groups=mesh['shard'=8,'tensor'=4] {'shard'}, dimensions={1}, use_global_device_ids=true | all-gather | bytes 589824 | tf_op jit(solution)/shard_map/all_gather | solution.py:73
  92.7 4.9 convolution_bitcast_fusion
  135.3 5.1 fusion.85
  144.2 16.4 %all-gather.1 = bf16[8,1,128]{2,1,0:T(2,128)(2,1)S(1)} all-gather(bf16[1,1,128]{2,1,0:T(2,128)(2,1)S(1)} %convert_bitcast_fusion), channel_id=1, replica_groups=mesh['shard'=8,'tensor'=4] {'shard'}, dimensions={0}, use_global_device_ids=true | all-gather | bytes 2304 | tf_op jit(solution)/shard_map/all_gather | solution.py:75
  160.6 100.0 %all-reduce.6.cloned.1.call-done = f32[1576,1024]{1,0:T(8,128)} async-done(((f32[1576,1024]{1,0:T(8,128)}), f32[1576,1024]{1,0:T(8,128)}) %all-reduce.6.cloned.1.call-update) | async-done | bytes 6455312 | tf_op jit(solution)/shard_map/psum | solution.py:104
  269.5 43.2 %all-gather.8.cloned.1.call-done = bf16[1024,1024]{1,0:T(8,128)(2,1)} async-done(((bf16[128,1024]{1,0:T(8,128)(2,1)}), bf16[1024,1024]{1,0:T(8,128)(2,1)}) %all-gather.8.cloned.1.call-update) | async-done | bytes 2097168 | tf_op jit(solution)/shard_map/all_gather | solution.py:74
  312.7 8.9 fusion.86
  321.5 42.5 %all-gather.10.cloned.1.call-done = bf16[1024,1024]{1,0:T(8,128)(2,1)} async-done(((bf16[1024,128]{1,0:T(8,128)(2,1)}), bf16[1024,1024]{1,0:T(8,128)(2,1)}) %all-gather.10.cloned.1.call-update) | async-done | bytes 2097168 | tf_op jit(solution)/shard_map/all_gather | solution.py:76
  364.0 21.1 %fusion.74 = (bf16[1024]{0:T(1024)(128)(2,1)S(1)}, bf16[1576,1024]{1,0:T(8,128)(2,1)S(1)}, f32[1576,1024]{1,0:T(8,128)}) fusion(f32[1576,1024]{1,0:T(8,128)} %fusion.86, f32[1024]{0:T(1024)S(1)} %bitcast.225, bf16[1576,1024]{1,0:T(8,128)(2,1)S(1)} %copy-done.7, bf16[1024,1024]{1,0:T(8,128)(2,1)} %all-gather.10.cloned.1.call-done), kind=kOutput, calls=%fused_computation.155 | convolution fusion | flops 3424533504 | bytes 21469184 | tf_op jit(solution)/shard_map/rd,fd->rf/dot_general | solution.py:118
  386.8 5.5 fusion.87
  392.6 9.3 multiply_convert_fusion.1
  401.9 111.0 %all-reduce.8.cloned.1.call-done = f32[1576,1024]{1,0:T(8,128)} async-done(((f32[1576,1024]{1,0:T(8,128)}), f32[1576,1024]{1,0:T(8,128)}) %all-reduce.8.cloned.1.call-update) | async-done | bytes 6455312 | tf_op jit(solution)/shard_map/psum | solution.py:125
  512.9 6.0 multiply_reduce_fusion.1
  519.5 4.6 fusion.76
  534.8 5.4 fusion.83
  544.9 6.3 multiply_convert_fusion
  554.3 8.3 convolution_convert_fusion.2
  566.6 8.3 convolution_convert_fusion.3
  575.1 6.5 fusion.41
  616.4 6.4 fusion.30
  643.0 21.5 %all-reduce = bf16[1024]{0:T(1024)(128)(2,1)S(1)} all-reduce(bf16[1024]{0:T(1024)(128)(2,1)S(1)} %get-tuple-element.138), channel_id=6, replica_groups=mesh['shard'=8,'tensor'=4] {'shard'}, use_global_device_ids=true, to_apply=%region_22.0.clone | all-reduce | flops 1024 | bytes 4096
  664.5 8.0 convolution_convert_fusion
  681.7 6.1 reduce-scatter.25.cloned.1.call-done
  689.0 70.1 %reduce-scatter.17.cloned.1.call-done = bf16[128,1024]{1,0:T(8,128)(2,1)} async-done(((bf16[1024,1024]{1,0:T(8,128)(2,1)}), bf16[128,1024]{1,0:T(8,128)(2,1)}) %reduce-scatter.17.cloned.1.call-update) | async-done | bytes 262160 | tf_op jit(solution)/shard_map/reduce_scatter | solution.py:197
  766.7 58.0 %reduce-scatter.23.cloned.1.call-done = bf16[128,256]{1,0:T(8,128)(2,1)} async-done(((bf16[1024,256]{1,0:T(8,128)(2,1)}), bf16[128,256]{1,0:T(8,128)(2,1)}) %reduce-scatter.23.cloned.1.call-update) | async-done | bytes 65552
  829.2 63.3 %reduce-scatter.19.cloned.1.call-done = bf16[128,768]{1,0:T(8,128)(2,1)} async-done(((bf16[1024,768]{1,0:T(8,128)(2,1)}), bf16[128,768]{1,0:T(8,128)(2,1)}) %reduce-scatter.19.cloned.1.call-update) | async-done | bytes 196624
  903.9 112.7 %all-reduce.10.cloned.1.call-done = (bf16[1576,1024]{1,0:T(8,128)(2,1)}, bf16[1576,1024]{1,0:T(8,128)(2,1)}) async-done(((bf16[1576,1024]{1,0:T(8,128)(2,1)}, bf16[1576,1024]{1,0:T(8,128)(2,1)}), (bf16[1576,1024]{1,0:T(8,128)(2,1)}, bf16[1576,1024]{1,0:T(8,128)(2,1)})) %all-reduce.10.cloned.1.call-update) | async-done | bytes 6455312 | tf_op jit(solution)/shard_map/psum | solution.py:114
  1026.2 8.3 fusion.73
  1035.5 6.7 add_convert_fusion.1
  1042.2 55.7 %reduce-scatter.27.cloned.1.call-done = bf16[128,6]{1,0:T(8,128)(2,1)} async-done(((bf16[1024,6]{1,0:T(8,128)(2,1)}), bf16[128,6]{1,0:T(8,128)(2,1)}) %reduce-scatter.27.cloned.1.call-update) | async-done | bytes 1552
  (258 shorter events, 184.2 us)
Async XLA Ops:
  7.2 55.8 %copy-start.2 = (bf16[1576,1024]{1,0:T(8,128)(2,1)S(1)}, bf16[1576,1024]{1,0:T(8,128)(2,1)}, u32[]{:S(2)}) copy-start(bf16[1576,1024]{1,0:T(8,128)(2,1)} %param.16) | copy-start | bytes 9682948
  7.2 85.5 %all-gather.6.cloned.1.call-start = ((), (), s32[]{:S(2)}) async-start(), calls=%async_computation.6 | async-start | bytes 1769472 | tf_op jit(solution)/shard_map/all_gather | solution.py:71
  9.1 251.5 %all-reduce.6.cloned.1.call-start = ((), (), s32[]{:S(2)}) async-start(), calls=%async_computation.7 | async-start | bytes 12910592 | tf_op jit(solution)/shard_map/psum | solution.py:104
  63.0 34.6 %copy-start.21 = (f32[1576]{0:T(1024)}, f32[1576]{0:T(1024)S(1)}, u32[]{:S(2)}) copy-start(f32[1576]{0:T(1024)S(1)} %broadcast_multiply_fusion.1) | copy-start | bytes 18916
  64.0 33.6 %copy-start.24 = (f32[1576]{0:T(1024)}, f32[1576]{0:T(1024)S(1)}, u32[]{:S(2)}) copy-start(f32[1576]{0:T(1024)S(1)} %fusion.60) | copy-start | bytes 18916
  64.6 33.0 %copy-start.29 = (f32[1,1024]{1,0:T(1,128)}, f32[1,1024]{1,0:T(1,128)S(1)}, u32[]{:S(2)}) copy-start(f32[1,1024]{1,0:T(1,128)S(1)} %get-tuple-element.164) | copy-start | bytes 12292
  64.6 33.0 %copy-start.44 = (f32[1,1024]{1,0:T(1,128)}, f32[1,1024]{1,0:T(1,128)S(1)}, u32[]{:S(2)}) copy-start(f32[1,1024]{1,0:T(1,128)S(1)} %get-tuple-element.165) | copy-start | bytes 12292
  140.4 172.2 %all-gather.8.cloned.1.call-start = ((), (), s32[]{:S(2)}) async-start(), calls=%async_computation.8 | async-start | bytes 2359296 | tf_op jit(solution)/shard_map/all_gather | solution.py:74
  142.3 221.8 %all-gather.10.cloned.1.call-start = ((), (), s32[]{:S(2)}) async-start(), calls=%async_computation.9 | async-start | bytes 2359296 | tf_op jit(solution)/shard_map/all_gather | solution.py:76
  144.1 368.8 %all-reduce.8.cloned.1.call-start = ((), (), s32[]{:S(2)}) async-start(), calls=%async_computation.10 | async-start | bytes 12910592 | tf_op jit(solution)/shard_map/psum | solution.py:125
  269.5 94.6 %copy-start.7 = (bf16[1576,1024]{1,0:T(8,128)(2,1)S(1)}, bf16[1576,1024]{1,0:T(8,128)(2,1)}, u32[]{:S(2)}) copy-start(bf16[1576,1024]{1,0:T(8,128)(2,1)} %param.17) | copy-start | bytes 9682948
  364.0 22.8 %copy-start.52 = (bf16[1024,1024]{1,0:T(8,128)(2,1)S(1)}, bf16[1024,1024]{1,0:T(8,128)(2,1)}, u32[]{:S(2)}) copy-start(bf16[1024,1024]{1,0:T(8,128)(2,1)} %all-gather.8.cloned.1.call-done) | copy-start | bytes 6291460
  392.3 287.4 %reduce-scatter.21.cloned.1.call-start = ((), (), s32[]{:S(2)}) async-start(), calls=%async_computation.13 | async-start | bytes 73728
  524.1 51.0 %copy-start.32 = (f32[1576]{0:T(1024)}, f32[1576]{0:T(1024)S(1)}, u32[]{:S(2)}) copy-start(f32[1576]{0:T(1024)S(1)} %negate_multiply_fusion.2) | copy-start | bytes 18916
  553.8 134.0 %reduce-scatter.25.cloned.1.call-start = ((), (), s32[]{:S(2)}) async-start(), calls=%async_computation.15 | async-start | bytes 2359296
  566.5 192.6 %reduce-scatter.17.cloned.1.call-start = ((), (), s32[]{:S(2)}) async-start(), calls=%async_computation.11 | async-start | bytes 2359296 | tf_op jit(solution)/shard_map/reduce_scatter | solution.py:197
  574.9 249.8 %reduce-scatter.23.cloned.1.call-start = ((), (), s32[]{:S(2)}) async-start(), calls=%async_computation.14 | async-start | bytes 589824
  598.5 17.8 %copy-start.25 = (f32[1576]{0:T(1024)S(1)}, f32[1576]{0:T(1024)}, u32[]{:S(2)}) copy-start(f32[1576]{0:T(1024)} %copy-done.24) | copy-start | bytes 18916
  598.5 17.8 %copy-start.30 = (f32[1,1024]{1,0:T(1,128)S(1)}, f32[1,1024]{1,0:T(1,128)}, u32[]{:S(2)}) copy-start(f32[1,1024]{1,0:T(1,128)} %copy-done.29) | copy-start | bytes 12292
  598.6 17.8 %copy-start.45 = (f32[1,1024]{1,0:T(1,128)S(1)}, f32[1,1024]{1,0:T(1,128)}, u32[]{:S(2)}) copy-start(f32[1,1024]{1,0:T(1,128)} %copy-done.44) | copy-start | bytes 12292
  612.1 280.4 %reduce-scatter.19.cloned.1.call-start = ((), (), s32[]{:S(2)}) async-start(), calls=%async_computation.12 | async-start | bytes 1769472
  626.9 37.6 %copy-start.47 = (f32[2,128]{1,0:T(2,128)S(1)}, f32[2,128]{1,0:T(2,128)}, u32[]{:S(2)}) copy-start(f32[2,128]{1,0:T(2,128)} %param.27) | copy-start | bytes 3076
  630.1 386.5 %all-reduce.10.cloned.1.call-start = ((), (), s32[]{:S(2)}) async-start(), calls=%async_computation.17 | async-start | bytes 12910592 | tf_op jit(solution)/shard_map/psum | solution.py:114
  676.8 421.1 %reduce-scatter.27.cloned.1.call-start = ((), (), s32[]{:S(2)}) async-start(), calls=%async_computation.16 | async-start | bytes 294912
  826.6 196.1 %copy-start.19 = (f32[256,128]{1,0:T(8,128)}, f32[256,128]{1,0:T(8,128)S(1)}, u32[]{:S(2)}) copy-start(f32[256,128]{1,0:T(8,128)S(1)} %get-tuple-element.133) | copy-start | bytes 393220
  898.5 120.6 %copy-start.23 = (f32[1576]{0:T(1024)S(1)}, f32[1576]{0:T(1024)}, u32[]{:S(2)}) copy-start(f32[1576]{0:T(1024)} %copy-done.21) | copy-start | bytes 18916
  898.5 120.6 %copy-start.31 = (f32[1,1024]{1,0:T(1,128)S(1)}, f32[1,1024]{1,0:T(1,128)}, u32[]{:S(2)}) copy-start(f32[1,1024]{1,0:T(1,128)} %copy-done.29) | copy-start | bytes 12292
  898.5 124.1 %copy-start.28 = (f32[1576]{0:T(1024)S(1)}, f32[1576]{0:T(1024)}, u32[]{:S(2)}) copy-start(f32[1576]{0:T(1024)} %copy-done.27) | copy-start | bytes 18916
  898.5 124.2 %copy-start.26 = (f32[1576]{0:T(1024)S(1)}, f32[1576]{0:T(1024)}, u32[]{:S(2)}) copy-start(f32[1576]{0:T(1024)} %copy-done.24) | copy-start | bytes 18916
  1035.5 63.3 %copy-start.34 = (f32[1,6,128]{2,0,1:T(1,128)S(1)}, f32[1,6,128]{2,0,1:T(1,128)}, u32[]{:S(2)}) copy-start(f32[1,6,128]{2,0,1:T(1,128)} %get-tuple-element.169) | copy-start | bytes 9220
  1035.5 63.3 %copy-start.39 = (f32[6,128]{1,0:T(8,128)S(1)}, f32[6,128]{1,0:T(8,128)}, u32[]{:S(2)}) copy-start(f32[6,128]{1,0:T(8,128)} %param.30) | copy-start | bytes 9220
  1035.5 63.3 %copy-start.41 = (f32[1,6,128]{2,0,1:T(1,128)S(1)}, f32[1,6,128]{2,0,1:T(1,128)}, u32[]{:S(2)}) copy-start(f32[1,6,128]{2,0,1:T(1,128)} %get-tuple-element.168) | copy-start | bytes 9220
  (38 other events, 240.9 us)
Sparse Core Ops, SparseCore 0:
  10.8 46.9 all-gather.5
  140.5 120.0 all-reduce.5
  263.3 49.2 all-gather.7
  315.1 48.8 all-gather.9
  392.4 120.4 all-reduce.7
  554.0 62.6 reduce-scatter.20
  620.2 67.5 reduce-scatter.24
  691.4 67.6 reduce-scatter.16
  763.0 61.6 reduce-scatter.22
  828.0 64.4 reduce-scatter.18
  895.5 121.0 all-reduce.9
  1035.6 62.2 reduce-scatter.26
where the time goes:
time: 1110 us
  waiting for transfers between devices  663 us (60%)
  blocking collectives  115 us (10%)
  local copies, waits for them, and re-layouts  109 us (10%)
  matrix products  108 us (10%)
  other arithmetic  94.5 us (9%)
  between operations  15.8 us (1%)
    unnamed x17, waiting for transfers between devices  183 us
    psum x1, waiting for transfers between devices, on_device(): lax.psum(shrink_term.astype(jnp.bfloat16), 'tensor').astype(jnp.float32)  113 us
    psum x1, waiting for transfers between devices, on_device(): mid_normed_grad = lax.psum(mid_part, 'tensor')  111 us
    psum x1, waiting for transfers between devices, on_device(): lax.psum(jnp.dot(context, full_output, preferred_element_type=jnp.float32...  100 us
    reduce_scatter x1, waiting for transfers between devices, on_device(): lax.psum_scatter(grad_expand.astype(jnp.bfloat16), 'shard', scatter_dimen...  70.1 us
    unnamed x138, local copies, waits for them, and re-layouts  46.1 us
    all_gather x1, waiting for transfers between devices, on_device(): lax.all_gather(expand_weight.astype(jnp.bfloat16), 'shard', axis=0, tiled...  43.2 us
    all_gather x1, waiting for transfers between devices, on_device(): lax.all_gather(shrink_weight.astype(jnp.bfloat16), 'shard', axis=1, tiled...  42.5 us
  transfers between devices with their start and end apart: 12, of which 10 were waited for; matrix products, arithmetic and copies ran while one was open for 15% of the time, Pallas kernels for 0%

commit v1 on v0

--- a/solution.py
+++ b/solution.py
@@ -122,7 +122,11 @@
     grad_expand = jnp.einsum("rd,rf->df", inputs_mid, pre_grad, preferred_element_type=jnp.float32)
     grad_expand_bias = jnp.sum(pre_grad.astype(jnp.float32), axis=0)
     mid_part = jnp.einsum("rf,df->rd", pre_grad, full_expand, preferred_element_type=jnp.float32)
-    mid_normed_grad = lax.psum(mid_part, "tensor")
+    mid_normed_grad = mid_part
+    for hop in (1, 2):
+        mid_normed_grad = mid_normed_grad + lax.ppermute(
+            mid_normed_grad, "tensor", [(dev, dev ^ hop) for dev in range(4)]
+        )
     mid_from_norm, gain_two, shift_two = second_back(mid_normed_grad)
     mid_grad = back_values + mid_from_norm
     mid_low = mid_grad.astype(jnp.bfloat16)

time: 1110 us -> 1020 us (0.919)
  waiting for transfers between devices: 663 us -> 573 us
    ppermute x0 -> x2, waiting for transfers between devices: none -> 124 us  [on_device(): lax.ppermute(mid_normed_grad, 'tensor', [(dev, dev ^ hop) for dev in rang...]
    psum x1 -> x0, waiting for transfers between devices: 111 us -> none  [on_device(): mid_normed_grad = lax.psum(mid_part, 'tensor')]
    reduce_scatter x1, waiting for transfers between devices: 70.1 us -> 0.02 us  [on_device(): lax.psum_scatter(grad_expand.astype(jnp.bfloat16), 'shard', scatter_dimen...]
    unnamed x17 -> x16, waiting for transfers between devices: 183 us -> 151 us
    unnamed x138 -> x140, local copies, waits for them, and re-layouts: 46.1 us -> 48.9 us
  transfers between devices with their start and end apart: 12 -> 13, of which waited for: 10 -> 9; matrix products, arithmetic and copies ran while one was open for 15% -> 20% of each run, Pallas kernels for 0% -> 0%
where the time goes in v1:
time: 1020 us
  waiting for transfers between devices  573 us (56%)
  blocking collectives  112 us (11%)
  local copies, waits for them, and re-layouts  109 us (11%)
  matrix products  107 us (10%)
  other arithmetic  96.1 us (9%)
  between operations  15.6 us (2%)
    unnamed x16, waiting for transfers between devices  151 us
    ppermute x2, waiting for transfers between devices, on_device(): lax.ppermute(mid_normed_grad, 'tensor', [(dev, dev ^ hop) for dev in rang...  124 us
    psum x1, waiting for transfers between devices, on_device(): lax.psum(shrink_term.astype(jnp.bfloat16), 'tensor').astype(jnp.float32)  113 us
    psum x1, waiting for transfers between devices, on_device(): lax.psum(jnp.dot(context, full_output, preferred_element_type=jnp.float32...  99.9 us
    unnamed x140, local copies, waits for them, and re-layouts  48.9 us
    all_gather x1, waiting for transfers between devices, on_device(): lax.all_gather(expand_weight.astype(jnp.bfloat16), 'shard', axis=0, tiled...  43.2 us
    all_gather x1, waiting for transfers between devices, on_device(): lax.all_gather(shrink_weight.astype(jnp.bfloat16), 'shard', axis=1, tiled...  42.5 us
    all_gather x1, blocking collectives, on_device(): lax.all_gather(output_weight.astype(jnp.bfloat16), 'shard', axis=1, tiled...  28.1 us
  transfers between devices with their start and end apart: 13, of which 9 were waited for; matrix products, arithmetic and copies ran while one was open for 20% of the time, Pallas kernels for 0%

profile of v1, /device:TPU:0, one launch (start us, length us, event | category | flops | bytes accessed | tf_op | source)
XLA Modules:
  0.0 1016.0 jit_solution(18152789051629115109)
XLA Ops:
  10.5 22.3 %all-gather = bf16[8,32,2]{1,2,0:T(2,128)(2,1)S(1)} all-gather(bf16[1,32,2]{1,2,0:T(2,128)(2,1)S(1)} %convert_bitcast_fusion.1), channel_id=1, replica_groups=mesh['shard'=8,'tensor'=4] {'shard'}, dimensions={0}, use_global_device_ids=true | all-gather | bytes 1152 | tf_op jit(solution)/shard_map/all_gather | solution.py:72
  34.0 26.5 %all_gather.21 = bf16[6,1024]{1,0:T(8,128)(2,1)S(1)} all-gather(bf16[6,128]{1,0:T(8,128)(2,1)S(1)} %convert_element_type.150), channel_id=1, replica_groups=mesh['shard'=8,'tensor'=4] {'shard'}, dimensions={1}, use_global_device_ids=true | all-gather | bytes 13824 | tf_op jit(solution)/shard_map/all_gather | solution.py:77
  64.6 28.1 %all_gather.24 = bf16[256,1024]{1,0:T(8,128)(2,1)} all-gather(bf16[256,128]{1,0:T(8,128)(2,1)S(1)} %convert_element_type.163), channel_id=1, replica_groups=mesh['shard'=8,'tensor'=4] {'shard'}, dimensions={1}, use_global_device_ids=true | all-gather | bytes 589824 | tf_op jit(solution)/shard_map/all_gather | solution.py:73
  92.7 4.9 convolution_bitcast_fusion
  134.9 5.1 fusion.85
  143.8 16.5 %all-gather.1 = bf16[8,1,128]{2,1,0:T(2,128)(2,1)S(1)} all-gather(bf16[1,1,128]{2,1,0:T(2,128)(2,1)S(1)} %convert_bitcast_fusion), channel_id=1, replica_groups=mesh['shard'=8,'tensor'=4] {'shard'}, dimensions={0}, use_global_device_ids=true | all-gather | bytes 2304 | tf_op jit(solution)/shard_map/all_gather | solution.py:75
  160.3 99.9 %all-reduce.5.cloned.1.call-done = f32[1576,1024]{1,0:T(8,128)} async-done(((f32[1576,1024]{1,0:T(8,128)}), f32[1576,1024]{1,0:T(8,128)}) %all-reduce.5.cloned.1.call-update) | async-done | bytes 6455312 | tf_op jit(solution)/shard_map/psum | solution.py:104
  269.1 43.2 %all-gather.8.cloned.1.call-done = bf16[1024,1024]{1,0:T(8,128)(2,1)} async-done(((bf16[128,1024]{1,0:T(8,128)(2,1)}), bf16[1024,1024]{1,0:T(8,128)(2,1)}) %all-gather.8.cloned.1.call-update) | async-done | bytes 2097168 | tf_op jit(solution)/shard_map/all_gather | solution.py:74
  312.3 8.9 fusion.86
  321.1 42.5 %all-gather.10.cloned.1.call-done = bf16[1024,1024]{1,0:T(8,128)(2,1)} async-done(((bf16[1024,128]{1,0:T(8,128)(2,1)}), bf16[1024,1024]{1,0:T(8,128)(2,1)}) %all-gather.10.cloned.1.call-update) | async-done | bytes 2097168 | tf_op jit(solution)/shard_map/all_gather | solution.py:76
  363.7 21.5 %fusion.74 = (bf16[1024]{0:T(1024)(128)(2,1)S(1)}, bf16[1576,1024]{1,0:T(8,128)(2,1)S(1)}, f32[1576,1024]{1,0:T(8,128)}) fusion(f32[1576,1024]{1,0:T(8,128)} %fusion.86, f32[1024]{0:T(1024)S(1)} %bitcast.225, bf16[1576,1024]{1,0:T(8,128)(2,1)S(1)} %copy-done.7, bf16[1024,1024]{1,0:T(8,128)(2,1)} %all-gather.10.cloned.1.call-done), kind=kOutput, calls=%fused_computation.155 | convolution fusion | flops 3424533504 | bytes 21469184 | tf_op jit(solution)/shard_map/rd,fd->rf/dot_general | solution.py:118
  390.6 10.4 %collective-permute-done = f32[1576,1024]{1,0:T(8,128)S(1)} collective-permute-done((f32[1576,1024]{1,0:T(8,128)S(1)}, f32[1576,1024]{1,0:T(8,128)S(1)}, u32[]{:S(2)}, u32[]{:S(2)}) %collective-permute-start) | collective-permute-done | bytes 6455328 | tf_op jit(solution)/shard_map/ppermute | solution.py:127
  406.7 6.4 multiply_convert_fusion.1
  414.8 5.3 convolution_convert_fusion.2
  424.2 8.2 convolution_convert_fusion.3
  432.7 113.9 %collective-permute-done.1 = f32[1576,1024]{1,0:T(8,128)} collective-permute-done((f32[1576,1024]{1,0:T(8,128)}, f32[1576,1024]{1,0:T(8,128)}, u32[]{:S(2)}, u32[]{:S(2)}) %collective-permute-start.1) | collective-permute-done | bytes 6455328 | tf_op jit(solution)/shard_map/ppermute | solution.py:127
  546.6 7.9 multiply_reduce_fusion.1
  554.5 4.7 fusion.76
  567.0 5.4 fusion.83
  572.5 7.9 multiply_reduce_fusion
  580.4 4.6 multiply_convert_fusion
  597.4 4.4 fusion.40
  601.8 5.6 fusion.41
  631.2 6.4 fusion.30
  657.8 18.7 %all-reduce = bf16[1024]{0:T(1024)(128)(2,1)S(1)} all-reduce(bf16[1024]{0:T(1024)(128)(2,1)S(1)} %get-tuple-element.138), channel_id=6, replica_groups=mesh['shard'=8,'tensor'=4] {'shard'}, use_global_device_ids=true, to_apply=%region_21.0.clone | all-reduce | flops 1024 | bytes 4096
  676.6 8.0 convolution_convert_fusion
  702.5 31.4 %reduce-scatter.23.cloned.1.call-done = bf16[128,256]{1,0:T(8,128)(2,1)} async-done(((bf16[1024,256]{1,0:T(8,128)(2,1)}), bf16[128,256]{1,0:T(8,128)(2,1)}) %reduce-scatter.23.cloned.1.call-update) | async-done | bytes 65552
  738.4 63.4 %reduce-scatter.19.cloned.1.call-done = bf16[128,768]{1,0:T(8,128)(2,1)} async-done(((bf16[1024,768]{1,0:T(8,128)(2,1)}), bf16[128,768]{1,0:T(8,128)(2,1)}) %reduce-scatter.19.cloned.1.call-update) | async-done | bytes 196624
  813.3 112.5 %all-reduce.7.cloned.1.call-done = (bf16[1576,1024]{1,0:T(8,128)(2,1)}, bf16[1576,1024]{1,0:T(8,128)(2,1)}) async-done(((bf16[1576,1024]{1,0:T(8,128)(2,1)}, bf16[1576,1024]{1,0:T(8,128)(2,1)}), (bf16[1576,1024]{1,0:T(8,128)(2,1)}, bf16[1576,1024]{1,0:T(8,128)(2,1)})) %all-reduce.7.cloned.1.call-update) | async-done | bytes 6455312 | tf_op jit(solution)/shard_map/psum | solution.py:114
  935.4 8.3 fusion.73
  944.8 6.7 add_convert_fusion.1
  951.4 55.7 %reduce-scatter.27.cloned.1.call-done = bf16[128,6]{1,0:T(8,128)(2,1)} async-done(((bf16[1024,6]{1,0:T(8,128)(2,1)}), bf16[128,6]{1,0:T(8,128)(2,1)}) %reduce-scatter.27.cloned.1.call-update) | async-done | bytes 1552
  (262 shorter events, 185.2 us)
Async XLA Ops:
  7.2 55.8 %copy-start.2 = (bf16[1576,1024]{1,0:T(8,128)(2,1)S(1)}, bf16[1576,1024]{1,0:T(8,128)(2,1)}, u32[]{:S(2)}) copy-start(bf16[1576,1024]{1,0:T(8,128)(2,1)} %param.16) | copy-start | bytes 9682948
  7.2 85.5 %all-gather.6.cloned.1.call-start = ((), (), s32[]{:S(2)}) async-start(), calls=%async_computation.6 | async-start | bytes 1769472 | tf_op jit(solution)/shard_map/all_gather | solution.py:71
  9.1 251.1 %all-reduce.5.cloned.1.call-start = ((), (), s32[]{:S(2)}) async-start(), calls=%async_computation.7 | async-start | bytes 12910592 | tf_op jit(solution)/shard_map/psum | solution.py:104
  63.0 34.6 %copy-start.22 = (f32[1576]{0:T(1024)}, f32[1576]{0:T(1024)S(1)}, u32[]{:S(2)}) copy-start(f32[1576]{0:T(1024)S(1)} %broadcast_multiply_fusion.1) | copy-start | bytes 18916
  64.0 33.6 %copy-start.25 = (f32[1576]{0:T(1024)}, f32[1576]{0:T(1024)S(1)}, u32[]{:S(2)}) copy-start(f32[1576]{0:T(1024)S(1)} %fusion.60) | copy-start | bytes 18916
  64.6 33.0 %copy-start.30 = (f32[1,1024]{1,0:T(1,128)}, f32[1,1024]{1,0:T(1,128)S(1)}, u32[]{:S(2)}) copy-start(f32[1,1024]{1,0:T(1,128)S(1)} %get-tuple-element.165) | copy-start | bytes 12292
  64.6 33.0 %copy-start.45 = (f32[1,1024]{1,0:T(1,128)}, f32[1,1024]{1,0:T(1,128)S(1)}, u32[]{:S(2)}) copy-start(f32[1,1024]{1,0:T(1,128)S(1)} %get-tuple-element.166) | copy-start | bytes 12292
  140.0 172.2 %all-gather.8.cloned.1.call-start = ((), (), s32[]{:S(2)}) async-start(), calls=%async_computation.8 | async-start | bytes 2359296 | tf_op jit(solution)/shard_map/all_gather | solution.py:74
  141.9 221.8 %all-gather.10.cloned.1.call-start = ((), (), s32[]{:S(2)}) async-start(), calls=%async_computation.9 | async-start | bytes 2359296 | tf_op jit(solution)/shard_map/all_gather | solution.py:76
  143.7 546.8 %reduce-scatter.25.cloned.1.call-start = ((), (), s32[]{:S(2)}) async-start(), calls=%async_computation.14 | async-start | bytes 2359296
  269.1 94.6 %copy-start.7 = (bf16[1576,1024]{1,0:T(8,128)(2,1)S(1)}, bf16[1576,1024]{1,0:T(8,128)(2,1)}, u32[]{:S(2)}) copy-start(bf16[1576,1024]{1,0:T(8,128)(2,1)} %param.17) | copy-start | bytes 9682948
  363.7 23.2 %copy-start.53 = (bf16[1024,1024]{1,0:T(8,128)(2,1)S(1)}, bf16[1024,1024]{1,0:T(8,128)(2,1)}, u32[]{:S(2)}) copy-start(bf16[1024,1024]{1,0:T(8,128)(2,1)} %all-gather.8.cloned.1.call-done) | copy-start | bytes 6291460
  390.5 10.5 %collective-permute-start = (f32[1576,1024]{1,0:T(8,128)S(1)}, f32[1576,1024]{1,0:T(8,128)S(1)}, u32[]{:S(2)}, u32[]{:S(2)}) collective-permute-start(f32[1576,1024]{1,0:T(8,128)S(1)} %fusion.87), channel_id=1, source_target_pairs={{0,1},{1,0},{2,3},{3,2},{4,5},{5,4},{6,7},{7,6},{8,9},{9,8},{10,11... | collective-permute-start | bytes 19365896 | tf_op jit(solution)/shard_map/ppermute | solution.py:127
  405.2 141.4 %collective-permute-start.1 = (f32[1576,1024]{1,0:T(8,128)}, f32[1576,1024]{1,0:T(8,128)}, u32[]{:S(2)}, u32[]{:S(2)}) collective-permute-start(f32[1576,1024]{1,0:T(8,128)} %add.265), channel_id=1, source_target_pairs={{0,2},{1,3},{2,0},{3,1},{4,6},{5,7},{6,4},{7,5},{8,10},{9,11},{10,... | collective-permute-start | bytes 19365896 | tf_op jit(solution)/shard_map/ppermute | solution.py:127
  424.1 267.6 %reduce-scatter.17.cloned.1.call-start = ((), (), s32[]{:S(2)}) async-start(), calls=%async_computation.10 | async-start | bytes 2359296 | tf_op jit(solution)/shard_map/reduce_scatter | solution.py:201
  432.4 268.1 %reduce-scatter.21.cloned.1.call-start = ((), (), s32[]{:S(2)}) async-start(), calls=%async_computation.12 | async-start | bytes 73728
  559.3 42.5 %copy-start.33 = (f32[1576]{0:T(1024)}, f32[1576]{0:T(1024)S(1)}, u32[]{:S(2)}) copy-start(f32[1576]{0:T(1024)S(1)} %negate_multiply_fusion.2) | copy-start | bytes 18916
  607.4 126.5 %reduce-scatter.23.cloned.1.call-start = ((), (), s32[]{:S(2)}) async-start(), calls=%async_computation.13 | async-start | bytes 589824
  611.6 19.6 %copy-start.46 = (f32[1,1024]{1,0:T(1,128)S(1)}, f32[1,1024]{1,0:T(1,128)}, u32[]{:S(2)}) copy-start(f32[1,1024]{1,0:T(1,128)} %copy-done.45) | copy-start | bytes 12292
  626.9 174.9 %reduce-scatter.19.cloned.1.call-start = ((), (), s32[]{:S(2)}) async-start(), calls=%async_computation.11 | async-start | bytes 1769472
  641.8 34.7 %copy-start.48 = (f32[2,128]{1,0:T(2,128)S(1)}, f32[2,128]{1,0:T(2,128)}, u32[]{:S(2)}) copy-start(f32[2,128]{1,0:T(2,128)} %param.27) | copy-start | bytes 3076
  645.0 280.8 %all-reduce.7.cloned.1.call-start = ((), (), s32[]{:S(2)}) async-start(), calls=%async_computation.16 | async-start | bytes 12910592 | tf_op jit(solution)/shard_map/psum | solution.py:114
  688.8 318.3 %reduce-scatter.27.cloned.1.call-start = ((), (), s32[]{:S(2)}) async-start(), calls=%async_computation.15 | async-start | bytes 294912
  701.3 32.6 %copy-start.47 = (f32[2,32]{1,0:T(2,128)}, f32[2,32]{1,0:T(2,128)S(1)}, u32[]{:S(2)}) copy-start(f32[2,32]{1,0:T(2,128)S(1)} %get-tuple-element.135) | copy-start | bytes 772
  735.8 196.1 %copy-start.20 = (f32[256,128]{1,0:T(8,128)}, f32[256,128]{1,0:T(8,128)S(1)}, u32[]{:S(2)}) copy-start(f32[256,128]{1,0:T(8,128)S(1)} %get-tuple-element.133) | copy-start | bytes 393220
  807.9 120.4 %copy-start.24 = (f32[1576]{0:T(1024)S(1)}, f32[1576]{0:T(1024)}, u32[]{:S(2)}) copy-start(f32[1576]{0:T(1024)} %copy-done.22) | copy-start | bytes 18916
  807.9 120.4 %copy-start.32 = (f32[1,1024]{1,0:T(1,128)S(1)}, f32[1,1024]{1,0:T(1,128)}, u32[]{:S(2)}) copy-start(f32[1,1024]{1,0:T(1,128)} %copy-done.30) | copy-start | bytes 12292
  807.9 124.0 %copy-start.29 = (f32[1576]{0:T(1024)S(1)}, f32[1576]{0:T(1024)}, u32[]{:S(2)}) copy-start(f32[1576]{0:T(1024)} %copy-done.28) | copy-start | bytes 18916
  807.9 124.0 %copy-start.27 = (f32[1576]{0:T(1024)S(1)}, f32[1576]{0:T(1024)}, u32[]{:S(2)}) copy-start(f32[1576]{0:T(1024)} %copy-done.25) | copy-start | bytes 18916
  944.7 63.3 %copy-start.35 = (f32[1,6,128]{2,0,1:T(1,128)S(1)}, f32[1,6,128]{2,0,1:T(1,128)}, u32[]{:S(2)}) copy-start(f32[1,6,128]{2,0,1:T(1,128)} %get-tuple-element.170) | copy-start | bytes 9220
  944.7 63.3 %copy-start.40 = (f32[6,128]{1,0:T(8,128)S(1)}, f32[6,128]{1,0:T(8,128)}, u32[]{:S(2)}) copy-start(f32[6,128]{1,0:T(8,128)} %param.30) | copy-start | bytes 9220
  944.7 63.3 %copy-start.42 = (f32[1,6,128]{2,0,1:T(1,128)S(1)}, f32[1,6,128]{2,0,1:T(1,128)}, u32[]{:S(2)}) copy-start(f32[1,6,128]{2,0,1:T(1,128)} %get-tuple-element.169) | copy-start | bytes 9220
  (40 other events, 302.3 us)
Sparse Core Ops, SparseCore 0:
  10.8 46.9 all-gather.5
  140.2 120.0 all-reduce.4
  262.9 49.2 all-gather.7
  314.8 48.8 all-gather.9
  424.2 65.5 reduce-scatter.24
  493.2 67.4 reduce-scatter.16
  607.5 60.7 reduce-scatter.20
  672.2 61.6 reduce-scatter.22
  737.3 64.4 reduce-scatter.18
  804.7 121.0 all-reduce.6
  944.8 62.2 reduce-scatter.26
